TPU v7x, 32 devices: a whole 2x2x4 slice. The times are simulated.
32 devices in a mesh: seq: 4 (over x, core), fsdp: 8 (over z, y).
Axes of the slice: x: 2, y: 2, z: 4, core: 2. Of those that a mesh axis runs over, the one named last changes fastest.
Arguments:
- query_in: bfloat16 [8, 512, 3072], P('fsdp', 'seq'), may hold values from -10 to 10
- key_in: bfloat16 [8, 512, 3072], P('fsdp', 'seq'), may hold values from -10 to 10
- value_in: bfloat16 [8, 512, 3072], P('fsdp', 'seq'), may hold values from -6 to 6
- positions: int32 [8, 512], P('fsdp', 'seq'), may hold values from 0 to 1023, as said below
- grad_out: bfloat16 [8, 512, 4096], P('fsdp', 'seq'), may hold values from -12 to 12
- out_weight: bfloat16 [3072, 4096], P('seq', 'fsdp'), may hold values from -0.109375 to 0.109375
Outputs:
- grad_query: bfloat16 [8, 512, 3072], P('fsdp', 'seq')
- grad_key: bfloat16 [8, 512, 3072], P('fsdp', 'seq')
- grad_value: bfloat16 [8, 512, 3072], P('fsdp', 'seq')
- grad_weight: float32 [3072, 4096], P('seq', 'fsdp')
Inputs may be any that keep to these rules, and one draw needn't show every extreme that they name: Within a clip the positions rise strictly; the first is 0 and the last is 1023.
All inputs are finite; a program needn't handle non-finite values.
Results may differ from a plain program's by a relative error of at most 0.004.
The roundings to bfloat16 on the way count: a program that leaves them out, or rounds other values in their place, can miss the bound.
Values may be sent and summed in bfloat16 or wider, within the bound.
No kernel may reach another device: no remote copies, remote signals or barrier semaphores. Data moves between devices by JAX's collectives and lax.ppermute only.
A program may use at most 128 MiB of HBM per device.

v0:
```python
import jax
import jax.numpy as jnp
from jax import lax
from jax.sharding import PartitionSpec as P

HEADS = 24
HD = 128


def rotary_tables(positions, head_dim):
    half_dim = head_dim // 2
    frequency = 10000.0 ** (-2.0 * jnp.arange(half_dim, dtype=jnp.float32) / head_dim)
    angles = positions.astype(jnp.float32)[:, None] * frequency[None, :]
    return (jnp.cos(angles), jnp.sin(angles))


def rotate(field, cosine_tab, sine_tab):
    half_dim = field.shape[-1] // 2
    front_half = field[..., :half_dim]
    back_half = field[..., half_dim:]
    cosine_b = cosine_tab[:, None, :]
    sine_b = sine_tab[:, None, :]
    return jnp.concatenate(
        [front_half * cosine_b - back_half * sine_b, front_half * sine_b + back_half * cosine_b],
        axis=-1,
    )


def unrotate(field, cosine_tab, sine_tab):
    half_dim = field.shape[-1] // 2
    front_half = field[..., :half_dim]
    back_half = field[..., half_dim:]
    cosine_b = cosine_tab[:, None, :]
    sine_b = sine_tab[:, None, :]
    return jnp.concatenate(
        [front_half * cosine_b + back_half * sine_b, back_half * cosine_b - front_half * sine_b],
        axis=-1,
    )


def attend_forward(inputs):
    query_head, key_head, value_head = inputs
    scores = jnp.dot(query_head, key_head.T, preferred_element_type=jnp.float32)
    row_top = jnp.max(scores, axis=1, keepdims=True)
    expo = jnp.exp(scores - row_top)
    attn_probs = expo / jnp.sum(expo, axis=1, keepdims=True)
    attended = jnp.dot(
        attn_probs.astype(jnp.bfloat16), value_head, preferred_element_type=jnp.float32
    ).astype(jnp.bfloat16)
    return (attn_probs, attended)


def attend_backward(inputs):
    attn_probs, query_head, key_head, value_head, grad_head = inputs
    factor = HD ** (-0.5)
    probs_low = attn_probs.astype(jnp.bfloat16)
    grad_value = jnp.dot(probs_low.T, grad_head, preferred_element_type=jnp.float32).astype(
        jnp.bfloat16
    )
    grad_probs = jnp.dot(grad_head, value_head.T, preferred_element_type=jnp.float32)
    row_delta = jnp.sum(attn_probs * grad_probs, axis=1, keepdims=True)
    grad_scores = (attn_probs * (grad_probs - row_delta)).astype(jnp.bfloat16)
    rot_grad_query = (
        jnp.dot(grad_scores, key_head, preferred_element_type=jnp.float32) * factor
    ).astype(jnp.bfloat16)
    rot_grad_key = jnp.dot(grad_scores.T, query_head, preferred_element_type=jnp.float32).astype(
        jnp.bfloat16
    )
    return (grad_value, rot_grad_query, rot_grad_key)


def sum_term(weight_term):
    return lax.psum_scatter(weight_term, "fsdp", scatter_dimension=1, tiled=True)


def shards(query_in, key_in, value_in, positions, grad_out, out_weight):
    tok_rows = query_in.shape[1]
    factor = HD ** (-0.5)
    cosine_tab, sine_tab = rotary_tables(positions[0], HD)
    rot_query = (
        rotate(query_in[0].astype(jnp.float32).reshape(tok_rows, HEADS, HD), cosine_tab, sine_tab)
        * factor
    ).astype(jnp.bfloat16)
    rot_key = rotate(
        key_in[0].astype(jnp.float32).reshape(tok_rows, HEADS, HD), cosine_tab, sine_tab
    ).astype(jnp.bfloat16)
    value_rows = value_in[0].reshape(tok_rows, HEADS, HD)
    query_rows, key_rows, value_all = (
        lax.all_to_all(rot_query, "seq", split_axis=1, concat_axis=0, tiled=True),
        lax.all_to_all(rot_key, "seq", split_axis=1, concat_axis=0, tiled=True),
        lax.all_to_all(value_rows, "seq", split_axis=1, concat_axis=0, tiled=True),
    )
    length = query_rows.shape[0]
    local_heads = query_rows.shape[1]
    head_width = local_heads * HD
    query_heads = query_rows.transpose(1, 0, 2)
    key_heads = key_rows.transpose(1, 0, 2)
    value_heads = value_all.transpose(1, 0, 2)
    attn_probs, attended = lax.map(attend_forward, (query_heads, key_heads, value_heads))
    attended_flat = attended.transpose(1, 0, 2).reshape(length, head_width)
    grad_local = grad_out[0]
    grad_all = lax.all_gather(grad_local, "seq", axis=0, tiled=True)
    grad_attended = jnp.dot(
        grad_all,
        lax.all_gather(out_weight, "fsdp", axis=1, tiled=True).T,
        preferred_element_type=jnp.float32,
    )
    grad_weight = sum_term(jnp.dot(attended_flat.T, grad_all, preferred_element_type=jnp.float32))
    grad_heads = (
        grad_attended.astype(jnp.bfloat16).reshape(length, local_heads, HD).transpose(1, 0, 2)
    )
    grad_value, rot_grad_query, rot_grad_key = lax.map(
        attend_backward, (attn_probs, query_heads, key_heads, value_heads, grad_heads)
    )
    back_value, back_query, back_key = (
        lax.all_to_all(
            grad_value.transpose(1, 0, 2), "seq", split_axis=0, concat_axis=1, tiled=True
        ),
        lax.all_to_all(
            rot_grad_query.transpose(1, 0, 2), "seq", split_axis=0, concat_axis=1, tiled=True
        ),
        lax.all_to_all(
            rot_grad_key.transpose(1, 0, 2), "seq", split_axis=0, concat_axis=1, tiled=True
        ),
    )
    grad_query = unrotate(back_query.astype(jnp.float32), cosine_tab, sine_tab).astype(jnp.bfloat16)
    grad_key = unrotate(back_key.astype(jnp.float32), cosine_tab, sine_tab).astype(jnp.bfloat16)
    flat_width = HEADS * HD
    return (
        grad_query.reshape(1, tok_rows, flat_width),
        grad_key.reshape(1, tok_rows, flat_width),
        back_value.reshape(1, tok_rows, flat_width),
        grad_weight,
    )


def solution(mesh):
    return jax.shard_map(
        shards,
        mesh=mesh,
        in_specs=(
            P("fsdp", "seq", None),
            P("fsdp", "seq", None),
            P("fsdp", "seq", None),
            P("fsdp", "seq"),
            P("fsdp", "seq", None),
            P("seq", "fsdp"),
        ),
        out_specs=(
            P("fsdp", "seq", None),
            P("fsdp", "seq", None),
            P("fsdp", "seq", None),
            P("seq", "fsdp"),
        ),
        check_vma=False,
    )
```

profile of v0, /device:TPU:0, one launch (start us, length us, event | category | flops | bytes accessed | tf_op | source)
XLA Modules:
  0.0 380.1 jit_solution(12657798446520250581)
XLA Ops:
  13.0 4.2 %all-to-all-start = ((bf16[128,24,128]{0,2,1:T(8,128)(2,1)}), bf16[128,24,128]{0,2,1:T(8,128)(2,1)S(1)}, u32[]{:S(2)}, u32[]{:S(2)}) async-start(bf16[128,24,128]{0,2,1:T(8,128)(2,1)} %fusion.44), calls=%async_computation | async-start | bytes 1572864 | tf_op jit(solution)/shard_map/all_to_all | solution.py:89
  18.2 17.5 %all-to-all-done = bf16[128,24,128]{0,2,1:T(8,128)(2,1)S(1)} async-done(((bf16[128,24,128]{0,2,1:T(8,128)(2,1)}), bf16[128,24,128]{0,2,1:T(8,128)(2,1)S(1)}, u32[]{:S(2)}, u32[]{:S(2)}) %all-to-all-start) | async-done | bytes 786464 | tf_op jit(solution)/shard_map/all_to_all | solution.py:89
  35.7 3.5 all-to-all-start.1
  39.2 1.2 copy.48
  40.4 19.3 %all-to-all-done.1 = bf16[128,24,128]{0,2,1:T(8,128)(2,1)S(1)} async-done(((bf16[128,24,128]{0,2,1:T(8,128)(2,1)}), bf16[128,24,128]{0,2,1:T(8,128)(2,1)S(1)}, u32[]{:S(2)}, u32[]{:S(2)}) %all-to-all-start.1) | async-done | bytes 786464 | tf_op jit(solution)/shard_map/all_to_all | solution.py:90
  59.6 3.5 all-to-all-start.2
  64.2 10.6 %all-to-all-done.2 = bf16[128,24,128]{0,2,1:T(8,128)(2,1)S(1)} async-done(((bf16[128,24,128]{0,2,1:T(8,128)(2,1)}), bf16[128,24,128]{0,2,1:T(8,128)(2,1)S(1)}, u32[]{:S(2)}, u32[]{:S(2)}) %all-to-all-start.2) | async-done | bytes 786464 | tf_op jit(solution)/shard_map/all_to_all | solution.py:91
  74.7 1.2 copy.50
  75.9 22.4 %while.26 = (s32[]{:T(128)}, f32[6,512,512]{1,2,0:T(8,128)}, bf16[6,512,128]{1,2,0:T(8,128)(2,1)}, bf16[6,512,128]{2,1,0:T(8,128)(2,1)S(1)}, bf16[6,512,128]{2,1...) while((s32[]{:T(128)}, f32[6,512,512]{1,2,0:T(8,128)}, bf16[6,512,128]{1,2,0:T(8,128)(2,1)}, ...), condition=%wide.region_3.4_spmd, body=%wide.region_0.3_spmd.sunk | while | flops 136379392 | bytes 6308429 | solution.py:99
  76.4 1.1 bitcast_dynamic-update-slice_fusion.2
  77.6 1.3 fusion.75
  80.1 1.1 bitcast_dynamic-update-slice_fusion.2
  81.2 1.3 fusion.75
  83.8 1.2 bitcast_dynamic-update-slice_fusion.2
  85.0 1.3 fusion.75
  87.6 1.1 bitcast_dynamic-update-slice_fusion.2
  88.7 1.3 fusion.75
  91.3 1.1 bitcast_dynamic-update-slice_fusion.2
  92.4 1.3 fusion.75
  95.0 1.2 bitcast_dynamic-update-slice_fusion.2
  96.2 1.3 fusion.75
  98.3 10.4 %fusion.40 = f32[768,4096]{1,0:T(8,128)} fusion(bf16[512,768]{0,1:T(8,128)(2,1)} %bitcast.179, bf16[1,512,4096]{2,1,0:T(8,128)(2,1)} %all-gather.6.cloned.1.call-done), kind=kOutput, calls=%fused_computation.48 | convolution fusion | flops 3221225472 | bytes 17563648 | tf_op jit(solution)/shard_map/dot_general | solution.py:108
  108.7 54.7 %all-gather.4.cloned.1.call-done = bf16[768,4096]{1,0:T(8,128)(2,1)} async-done(((bf16[768,512]{1,0:T(8,128)(2,1)}), bf16[768,4096]{1,0:T(8,128)(2,1)}) %all-gather.4.cloned.1.call-update) | async-done | bytes 6291472 | tf_op jit(solution)/shard_map/all_gather | solution.py:105
  163.4 8.5 %fusion.45 = bf16[512,768]{1,0:T(8,128)(2,1)} fusion(bf16[768,4096]{1,0:T(8,128)(2,1)} %all-gather.4.cloned.1.call-done, bf16[1,512,4096]{2,1,0:T(8,128)(2,1)} %all-gather.6.cloned.1.call-done), kind=kOutput, calls=%fused_computation.56 | convolution fusion | flops 3221618688 | bytes 11272192 | tf_op jit(solution)/shard_map/dot_general | solution.py:103
  171.8 1.6 copy.51
  173.4 40.2 %while.27 = (s32[]{:T(128)}, bf16[6,512,128]{2,1,0:T(8,128)(2,1)S(1)}, bf16[6,512,128]{2,1,0:T(8,128)(2,1)}, bf16[6,512,128]{2,1,0:T(8,128)(2,1)}, f32[6,512,512...) while((s32[]{:T(128)}, ...), condition=%wide.region_6.7_spmd, body=%wide.region_4.6_spmd.sunk | while | flops 270007808 | bytes 7349353 | solution.py:112
  173.4 1.7 fusion.83
  175.1 1.5 fusion.84
  178.5 1.6 fusion.82
  180.1 1.6 fusion.83
  181.7 1.5 fusion.84
  185.2 1.6 fusion.82
  186.8 1.6 fusion.83
  188.4 1.5 fusion.84
  191.9 1.6 fusion.82
  193.5 1.6 fusion.83
  195.1 1.5 fusion.84
  198.6 1.6 fusion.82
  200.2 1.6 fusion.83
  201.8 1.5 fusion.84
  205.3 1.6 fusion.82
  206.8 1.7 fusion.83
  208.5 1.5 fusion.84
  212.0 1.6 fusion.82
  213.6 2.7 copy.86
  216.3 3.5 all-to-all-start.3
  219.8 1.6 copy.85
  221.4 12.8 %all-to-all-done.3 = bf16[512,6,128]{2,1,0:T(8,128)(2,1)S(1)} async-done(((bf16[512,6,128]{2,1,0:T(8,128)(2,1)}), bf16[512,6,128]{2,1,0:T(8,128)(2,1)S(1)}, u32[]{:S(2)}, u32[]{:S(2)}) %all-to-all-start.3) | async-done | bytes 786464 | tf_op jit(solution)/shard_map/all_to_all | solution.py:119
  234.2 3.5 all-to-all-start.4
  237.7 1.5 copy.84
  239.7 12.4 %all-to-all-done.4 = bf16[512,6,128]{2,1,0:T(8,128)(2,1)S(1)} async-done(((bf16[512,6,128]{2,1,0:T(8,128)(2,1)}), bf16[512,6,128]{2,1,0:T(8,128)(2,1)S(1)}, u32[]{:S(2)}, u32[]{:S(2)}) %all-to-all-start.4) | async-done | bytes 786464 | tf_op jit(solution)/shard_map/all_to_all | solution.py:122
  252.1 4.5 %all-to-all-start.5 = ((bf16[512,6,128]{2,1,0:T(8,128)(2,1)}), bf16[512,6,128]{2,1,0:T(8,128)(2,1)}, u32[]{:S(2)}, u32[]{:S(2)}) async-start(bf16[512,6,128]{2,1,0:T(8,128)(2,1)} %bitcast.123), calls=%async_computation.5 | async-start | bytes 2097152 | tf_op jit(solution)/shard_map/all_to_all | solution.py:116
  257.0 1.8 fusion.50
  258.8 1.7 fusion.49
  260.5 2.7 copy.77
  263.3 1.3 copy.78
  264.6 2.7 copy.79
  267.4 1.3 copy.80
  268.8 1.8 add_convert_fusion
  270.7 1.2 copy.67
  271.9 1.2 copy.68
  273.0 1.6 copy.65
  274.7 1.2 copy.69
  275.8 97.8 %reduce-scatter.2.cloned.1.call-done = f32[768,512]{1,0:T(8,128)} async-done(((f32[768,4096]{1,0:T(8,128)}), f32[768,512]{1,0:T(8,128)}) %reduce-scatter.2.cloned.1.call-update) | async-done | bytes 1572880 | tf_op jit(solution)/shard_map/reduce_scatter | solution.py:73
  (82 shorter events, 28.2 us)
Async XLA Ops:
  7.2 1.5 copy-start.3
  7.2 91.1 %all-gather.6.cloned.1.call-start = ((), (), s32[]{:S(2)}) async-start(), calls=%async_computation.9 | async-start | bytes 5242880 | tf_op jit(solution)/shard_map/all_gather | solution.py:102
  7.9 155.5 %all-gather.4.cloned.1.call-start = ((), (), s32[]{:S(2)}) async-start(), calls=%async_computation.7 | async-start | bytes 7077888 | tf_op jit(solution)/shard_map/all_gather | solution.py:105
  9.0 1.1 copy-start.4
  10.6 0.7 copy-start.6
  13.0 22.7 %all-to-all-start = ((bf16[128,24,128]{0,2,1:T(8,128)(2,1)}), bf16[128,24,128]{0,2,1:T(8,128)(2,1)S(1)}, u32[]{:S(2)}, u32[]{:S(2)}) async-start(bf16[128,24,128]{0,2,1:T(8,128)(2,1)} %fusion.44), calls=%async_computation | async-start | bytes 1572864 | tf_op jit(solution)/shard_map/all_to_all | solution.py:89
  17.2 22.0 %copy-start.5 = (bf16[1,128,3072]{2,1,0:T(8,128)(2,1)S(1)}, bf16[1,128,3072]{2,1,0:T(8,128)(2,1)}, u32[]{:S(2)}) copy-start(bf16[1,128,3072]{2,1,0:T(8,128)(2,1)} %param.12) | copy-start | bytes 2359300
  35.7 23.9 %all-to-all-start.1 = ((bf16[128,24,128]{0,2,1:T(8,128)(2,1)}), bf16[128,24,128]{0,2,1:T(8,128)(2,1)S(1)}, u32[]{:S(2)}, u32[]{:S(2)}) async-start(bf16[128,24,128]{0,2,1:T(8,128)(2,1)} %pad_maximum_fusion), calls=%async_computation.1 | async-start | bytes 1572864 | tf_op jit(solution)/shard_map/all_to_all | solution.py:90
  59.6 15.1 %all-to-all-start.2 = ((bf16[128,24,128]{0,2,1:T(8,128)(2,1)}), bf16[128,24,128]{0,2,1:T(8,128)(2,1)S(1)}, u32[]{:S(2)}, u32[]{:S(2)}) async-start(bf16[128,24,128]{0,2,1:T(8,128)(2,1)} %bitcast.29), calls=%async_computation.2 | async-start | bytes 1572864 | tf_op jit(solution)/shard_map/all_to_all | solution.py:91
  63.1 310.5 %reduce-scatter.2.cloned.1.call-start = ((), (), s32[]{:S(2)}) async-start(), calls=%async_computation.8 | async-start | bytes 14155776 | tf_op jit(solution)/shard_map/reduce_scatter | solution.py:73
  213.6 6.3 %copy-start.2 = (bf16[6,512,128]{2,1,0:T(8,128)(2,1)S(1)}, bf16[6,512,128]{2,1,0:T(8,128)(2,1)}, u32[]{:S(2)}) copy-start(bf16[6,512,128]{2,1,0:T(8,128)(2,1)} %get-tuple-element.88) | copy-start | bytes 2359300
  216.3 17.9 %all-to-all-start.3 = ((bf16[512,6,128]{2,1,0:T(8,128)(2,1)}), bf16[512,6,128]{2,1,0:T(8,128)(2,1)S(1)}, u32[]{:S(2)}, u32[]{:S(2)}) async-start(bf16[512,6,128]{2,1,0:T(8,128)(2,1)} %bitcast.125), calls=%async_computation.3 | async-start | bytes 2097152 | tf_op jit(solution)/shard_map/all_to_all | solution.py:119
  234.2 17.9 %all-to-all-start.4 = ((bf16[512,6,128]{2,1,0:T(8,128)(2,1)}), bf16[512,6,128]{2,1,0:T(8,128)(2,1)S(1)}, u32[]{:S(2)}, u32[]{:S(2)}) async-start(bf16[512,6,128]{2,1,0:T(8,128)(2,1)} %bitcast.167), calls=%async_computation.4 | async-start | bytes 2097152 | tf_op jit(solution)/shard_map/all_to_all | solution.py:122
  252.1 20.9 %all-to-all-start.5 = ((bf16[512,6,128]{2,1,0:T(8,128)(2,1)}), bf16[512,6,128]{2,1,0:T(8,128)(2,1)}, u32[]{:S(2)}, u32[]{:S(2)}) async-start(bf16[512,6,128]{2,1,0:T(8,128)(2,1)} %bitcast.123), calls=%async_computation.5 | async-start | bytes 2097152 | tf_op jit(solution)/shard_map/all_to_all | solution.py:116
  267.3 1.3 copy-start
  267.4 1.4 copy-start.1
Sparse Core Ops, SparseCore 0:
  9.5 51.7 all-gather.5
  63.4 99.9 all-gather.3
  167.5 206.0 reduce-scatter.1
where the time goes:
time: 382 us; the launch traced here: 380 us
  waiting for transfers between devices  226 us (59%)
  matrix products  59.3 us (16%)
  local copies, waits for them, and re-layouts  34.7 us (9%)
  starting transfers between devices  23 us (6%)
  other arithmetic  22.3 us (6%)
  between operations  14 us (4%)
    reduce_scatter x1, waiting for transfers between devices, sum_term(): lax.psum_scatter(weight_term, 'fsdp', scatter_dimension=1, tiled=True)  97.8 us
    all_gather x1, waiting for transfers between devices, shards(): lax.all_gather(out_weight, 'fsdp', axis=1, tiled=True)  54.7 us
    all_to_all x1, waiting for transfers between devices, shards(): lax.all_to_all(rot_key, 'seq', split_axis=1, concat_axis=0, tiled=True)  19.3 us
    all_to_all x1, waiting for transfers between devices, shards(): lax.all_to_all(rot_query, 'seq', split_axis=1, concat_axis=0, tiled=True)  17.5 us
    unnamed x24, local copies, waits for them, and re-layouts  15.1 us
    all_to_all x1, waiting for transfers between devices, shards(): lax.all_to_all(rot_grad_query.transpose(1, 0, 2), 'seq', split_axis=0, co...  12.8 us
    all_to_all x1, waiting for transfers between devices, shards(): lax.all_to_all(rot_grad_key.transpose(1, 0, 2), 'seq', split_axis=0, conc...  12.4 us
    all_to_all x1, waiting for transfers between devices, shards(): lax.all_to_all(value_rows, 'seq', split_axis=1, concat_axis=0, tiled=True)  10.6 us
  transfers between devices with their start and end apart: 9, of which 7 were waited for; matrix products, arithmetic and copies ran while one was open for 30% of the time, Pallas kernels for 0%

commit v1 on v0

v1 whole, which is shorter than its diff:
```python
import jax
import jax.numpy as jnp
from jax import lax
from jax.experimental import pallas as pl
from jax.experimental.pallas import tpu as pltpu
from jax.sharding import PartitionSpec as P


HD = 128
CHUNKS = 3
BF = jnp.bfloat16
F32 = jnp.float32
VMEM_LIMIT = 16 * 1024 * 1024


NT = (((1,), (1,)), ((), ()))
TN = (((0,), (0,)), ((), ()))
NN = (((1,), (0,)), ((), ()))


def mm(a, b, dims):
    return lax.dot_general(a, b, dims, preferred_element_type=F32)


def call(kernel, outs, flops, nbytes, **kw):
    return pl.pallas_call(
        kernel,
        out_shape=outs,
        compiler_params=pltpu.CompilerParams(vmem_limit_bytes=VMEM_LIMIT),
        cost_estimate=pl.CostEstimate(flops=int(flops), bytes_accessed=int(nbytes), transcendentals=0),
        **kw,
    )


def whole():
    return pl.BlockSpec(memory_space=pltpu.VMEM)


def smem():
    return pl.BlockSpec(memory_space=pltpu.SMEM)


def bits_of(n):
    assert n & (n - 1) == 0
    return [1 << i for i in range(n.bit_length() - 1)]


def split_columns(grad, blocks, order, pair):
    tok, width = grad.shape
    step = width // blocks

    def kernel(at, g, own, other):
        for j, m in enumerate(order):
            for base, out in ((at[1], own), (at[1] ^ pair, other)):
                start = pl.multiple_of((base ^ m) * step, step)
                out[:, j * step : (j + 1) * step] = g[:, pl.ds(start, step)]

    def run(at):
        shape = jax.ShapeDtypeStruct((tok, width // 2), grad.dtype)
        return call(
            kernel, (shape, shape), 0, 4 * grad.size,
            in_specs=[smem(), whole()], out_specs=(whole(), whole()),
        )(at, grad)

    return run


def cut_heads(query, key, value, cosine, sine, at, seq, sizes):
    tok, width = query.shape
    rows = width // seq
    factor = HD ** (-0.5)

    def kernel(at_ref, q, k, v, cos, sin, *outs):
        c, s = cos[...], sin[...]
        for part in range(seq):
            start = (at_ref[0] ^ part) * rows
            head = 0
            for j, size in enumerate(sizes):
                out = outs[j * seq + part]
                for h in range(size):
                    cols = pl.ds(pl.multiple_of(start + head * HD, HD), HD)
                    x = q[:, cols].astype(F32)
                    out[h, 0] = ((x * c + pltpu.roll(x, HD // 2, 1) * s) * factor).astype(BF)
                    x = k[:, cols].astype(F32)
                    out[h, 1] = (x * c + pltpu.roll(x, HD // 2, 1) * s).astype(BF)
                    out[h, 2] = v[:, cols]
                    head += 1

    outs = [jax.ShapeDtypeStruct((n, 3, tok, HD), BF) for n in sizes for _ in range(seq)]
    res = call(
        kernel, outs, 0, 12 * query.size,
        in_specs=[smem()] + [whole()] * 5, out_specs=[whole()] * len(outs),
    )(at, query, key, value, cosine, sine)
    return [list(res[j * seq : (j + 1) * seq]) for j in range(len(sizes))]


def gathered(refs, head, which):
    return jnp.concatenate([r[head, which] for r in refs], axis=0)


def probs_of(query, key):
    scores = mm(key, query, NT)
    expo = jnp.exp(scores - jnp.max(scores, axis=0, keepdims=True))
    return expo * (1.0 / jnp.sum(expo, axis=0, keepdims=True))


def attend(parts):
    count, _, tok, _ = parts[0].shape
    length = tok * len(parts)

    def kernel(*refs):
        ins, out = refs[:-1], refs[-1]
        for h in range(count):
            low = probs_of(gathered(ins, h, 0), gathered(ins, h, 1)).astype(BF)
            out[h * HD : (h + 1) * HD] = mm(gathered(ins, h, 2), low, TN).astype(BF)

    return call(
        kernel, jax.ShapeDtypeStruct((count * HD, length), BF),
        4 * count * length * length * HD, 8 * count * length * HD,
        in_specs=[whole()] * len(parts), out_specs=whole(),
    )(*parts)


def attend_back(parts, mine, theirs):
    count, _, tok, _ = parts[0].shape
    length = tok * len(parts)
    factor = HD ** (-0.5)
    seq = len(parts)

    def kernel(*refs):
        ins, (a, b), outs = refs[:seq], refs[seq : seq + 2], refs[seq + 2 :]
        for h in range(count):
            cols = slice(h * HD, (h + 1) * HD)
            query, key, value = (gathered(ins, h, i) for i in range(3))
            grad = (a[:, cols] + b[:, cols].astype(F32)).astype(BF)
            probs = probs_of(query, key)
            grad_value = mm(probs.astype(BF), grad, NN)
            grad_probs = mm(value, grad, NT)
            delta = jnp.sum(probs * grad_probs, axis=0, keepdims=True)
            grad_scores = (probs * (grad_probs - delta)).astype(BF)
            grad_key = mm(grad_scores, query, NN)
            grad_query = (mm(key, grad_scores, TN) * factor).T
            for i, out in enumerate(outs):
                at = slice(i * tok, (i + 1) * tok)
                out[h, 0] = grad_query[at].astype(BF)
                out[h, 1] = grad_key[at].astype(BF)
                out[h, 2] = grad_value[at].astype(BF)

    return list(call(
        kernel, [jax.ShapeDtypeStruct(parts[0].shape, BF)] * seq,
        12 * count * length * length * HD, 20 * count * length * HD,
        in_specs=[whole()] * (seq + 2), out_specs=[whole()] * seq,
    )(*parts, mine, theirs))


def rows_of(refs, cols):
    return jnp.concatenate([r[:, cols] for r in refs], axis=0)


def project_back(grads, weights, kind):
    count, blocks = len(grads), len(weights)
    tok, width = grads[0].shape
    rows, step = weights[0].shape
    total = tok * count
    half = total // 2

    def kernel(*refs):
        grad_refs, weight_refs = refs[:count], refs[count : count + blocks]
        mine, theirs = refs[count + blocks :]
        acc = None
        for j in range(blocks):
            left = rows_of(grad_refs, slice(j * step, (j + 1) * step))
            term = mm(left, weight_refs[j][...], NT)
            acc = term if acc is None else acc + term
        mine[...] = acc[:half]
        theirs[...] = acc[half:].astype(kind)

    return call(
        kernel,
        (jax.ShapeDtypeStruct((half, rows), F32), jax.ShapeDtypeStruct((half, rows), kind)),
        2 * total * width * rows, 2 * total * width + 2 * rows * width + 6 * half * rows,
        in_specs=[whole()] * (count + blocks), out_specs=(whole(), whole()),
    )(*grads, *weights)


def weight_terms(grads, mine, theirs, types):
    count, blocks = len(grads), len(types)
    tok, width = grads[0].shape
    rows, _ = mine.shape
    step = width // blocks
    total = tok * count

    def kernel(*refs):
        grad_refs, (a, b), outs = refs[:count], refs[count : count + 2], refs[count + 2 :]
        left = jnp.concatenate([a[...], b[...]], axis=1)
        for j in range(blocks):
            right = rows_of(grad_refs, slice(j * step, (j + 1) * step))
            outs[j][...] = mm(left, right, NN).astype(outs[j].dtype)

    return list(call(
        kernel, [jax.ShapeDtypeStruct((rows, step), t) for t in types],
        2 * total * width * rows, 2 * total * width + 4 * rows * width,
        in_specs=[whole()] * (count + 2), out_specs=[whole()] * blocks,
    )(*grads, mine, theirs))


def join_heads(chunks, cosine, sine, at, seq, sizes):
    tok = cosine.shape[0]
    rows = sum(sizes) * HD
    width = rows * seq

    def kernel(at_ref, cos, sin, *refs):
        ins, outs = refs[:-3], refs[-3:]
        c, s = cos[...], sin[...]
        for part in range(seq):
            start = (at_ref[0] ^ part) * rows
            head = 0
            for j, size in enumerate(sizes):
                src = ins[j * seq + part]
                for h in range(size):
                    cols = pl.ds(pl.multiple_of(start + head * HD, HD), HD)
                    for i in range(2):
                        x = src[h, i].astype(F32)
                        outs[i][:, cols] = (x * c - pltpu.roll(x, HD // 2, 1) * s).astype(BF)
                    outs[2][:, cols] = src[h, 2]
                    head += 1

    flat = [x for chunk in chunks for x in chunk]
    shape = jax.ShapeDtypeStruct((tok, width), BF)
    return call(
        kernel, (shape, shape, shape), 0, 12 * tok * width,
        in_specs=[smem()] + [whole()] * (2 + len(flat)), out_specs=(whole(),) * 3,
    )(at, cosine, sine, *flat)


def rotary_tables(positions):
    half = HD // 2
    frequency = 10000.0 ** (-2.0 * jnp.arange(half, dtype=F32) / HD)
    angles = positions.astype(F32)[:, None] * frequency[None, :]
    cosine, sine = jnp.cos(angles), jnp.sin(angles)
    return jnp.concatenate([cosine, cosine], 1), jnp.concatenate([-sine, sine], 1)


def shards(seq, fsdp, query_in, key_in, value_in, positions, grad_out, out_weight):
    query, key, value, grad = query_in[0], key_in[0], value_in[0], grad_out[0]
    seq_bits, clip_bits = bits_of(seq), bits_of(fsdp)
    pair = clip_bits[0]
    rest = [b for b in clip_bits if b != pair]
    order = [0]
    for bit in reversed(rest):
        order += [m | bit for m in order]
    heads = query.shape[1] // HD // seq
    chunks = min(CHUNKS, heads)
    sizes = [heads // chunks + (j < heads % chunks) for j in range(chunks)]
    edges = [sum(sizes[:j]) * HD for j in range(chunks + 1)]

    at = jnp.stack([lax.axis_index("seq"), lax.axis_index("fsdp")]).astype(jnp.int32)

    def send(x, axis, bit):
        n = {"seq": seq, "fsdp": fsdp}[axis]
        return lax.ppermute(x, axis, [(i, i ^ bit) for i in range(n)])

    split = split_columns(grad, fsdp, order, pair)
    own, other = split(at)
    grads = [{0: own}, {0: send(other, "fsdp", pair)}]
    for held in grads:
        for bit in reversed(seq_bits):
            for m in list(held):
                held[m | bit] = send(held[m], "seq", bit)
    sides = [held[m] for held in grads for m in range(seq)]

    weights = []
    for j in range(chunks):
        held = {0: out_weight[edges[j] : edges[j + 1]]}
        for bit in reversed(rest):
            for m in list(held):
                held[m | bit] = send(held[m], "fsdp", bit)
        weights.append([held[m] for m in order])

    cosine, sine = rotary_tables(positions[0])
    parts = cut_heads(query, key, value, cosine, sine, at, seq, sizes)
    parts = [[p if m == 0 else send(p, "seq", m) for m, p in enumerate(c)] for c in parts]

    types = [BF if rest and m & rest[0] else F32 for m in order]
    back, grad_weight = [], []
    for j in range(chunks):
        mine = attend(parts[j])
        theirs = send(mine, "fsdp", pair)
        terms = dict(zip(order, weight_terms(sides, mine, theirs, types)))
        for bit in rest:
            for m in [m for m in order if m & bit and m in terms]:
                got = send(terms.pop(m).astype(BF), "fsdp", bit)
                terms[m ^ bit] = terms[m ^ bit] + got.astype(F32)
        grad_weight.append(terms[0])

        kind = F32
        near, far = project_back(sides, weights[j], kind)
        far = send(far, "fsdp", pair)
        grads_back = attend_back(parts[j], near, far)
        back.append([g if m == 0 else send(g, "seq", m) for m, g in enumerate(grads_back)])

    outs = join_heads(back, cosine, sine, at, seq, sizes)
    return (*(o[None] for o in outs), jnp.concatenate(grad_weight, 0))


def solution(mesh):
    tokens = P("fsdp", "seq", None)

    def body(*args):
        return shards(mesh.shape["seq"], mesh.shape["fsdp"], *args)

    return jax.shard_map(
        body,
        mesh=mesh,
        in_specs=(tokens, tokens, tokens, P("fsdp", "seq"), tokens, P("seq", "fsdp")),
        out_specs=(tokens, tokens, tokens, P("seq", "fsdp")),
        check_vma=False,
    )
```

time: 382 us -> 192 us (0.50)
  waiting for transfers between devices: 226 us -> 105 us
  matrix products: 59.3 us -> 0 us
  starting transfers between devices: 23 us -> 56.7 us
  local copies, waits for them, and re-layouts: 34.7 us -> 2.42 us
  Pallas kernels: 0 us -> 22.9 us
  other arithmetic: 22.3 us -> 2.93 us
  between operations: 14 us -> 0.94 us
    ppermute x0 -> x49, waiting for transfers between devices: none -> 105 us  [send(): return lax.ppermute(x, axis, [(i, i ^ bit) for i in range(n)])]
    reduce_scatter x1 -> x0, waiting for transfers between devices: 97.8 us -> none  [sum_term(): lax.psum_scatter(weight_term, 'fsdp', scatter_dimension=1, tiled=True)]
    all_to_all x6 -> x0, waiting for transfers between devices: 72.6 us -> none  [the longest x1 19.3 us: shards(): lax.all_to_all(rot_key, 'seq', split_axis=1, concat_axis=0, tiled=True)]
    dot_general x38 -> x0, matrix products: 59.3 us -> none  [the longest x1 10.4 us: shards(): jnp.dot(attended_flat.T, grad_all, preferred_element_type=jnp.float32)]
    ppermute x0 -> x49, starting transfers between devices: none -> 56.7 us  [send(): return lax.ppermute(x, axis, [(i, i ^ bit) for i in range(n)])]
    all_gather x2 -> x0, waiting for transfers between devices: 54.7 us -> none  [the longest x1 54.7 us: shards(): lax.all_gather(out_weight, 'fsdp', axis=1, tiled=True)]
    pallas_call x0 -> x15, Pallas kernels: none -> 22.9 us  [the longest x3 6.42 us: attend_back(): call(kernel, [jax.ShapeDtypeStruct(parts[0].shape, BF)] * seq, 12 * count...]
    all_to_all x6 -> x0, starting transfers between devices: 22.7 us -> none  [the longest x1 4.48 us: shards(): lax.all_to_all(grad_value.transpose(1, 0, 2), 'seq', split_axis=0, concat...]
  transfers between devices with their start and end apart: 9 -> 49, of which waited for: 7 -> 25; matrix products, arithmetic and copies ran while one was open for 30% -> 2% of each run, Pallas kernels for 0% -> 10%
where the time goes in v1:
time: 192 us; the launch traced here: 191 us
  waiting for transfers between devices  105 us (55%)
  starting transfers between devices  56.7 us (30%)
  Pallas kernels  22.9 us (12%)
  other arithmetic  2.93 us (2%)
  local copies, waits for them, and re-layouts  2.42 us (1%)
    ppermute x49, waiting for transfers between devices, send(): return lax.ppermute(x, axis, [(i, i ^ bit) for i in range(n)])  105 us
    ppermute x49, starting transfers between devices, send(): return lax.ppermute(x, axis, [(i, i ^ bit) for i in range(n)])  56.7 us
    pallas_call x3, Pallas kernels, attend_back(): call(kernel, [jax.ShapeDtypeStruct(parts[0].shape, BF)] * seq, 12 * count...  6.42 us
    pallas_call x3, Pallas kernels, project_back(): call(kernel, (jax.ShapeDtypeStruct((half, rows), F32), jax.ShapeDtypeStru...  4.02 us
  transfers between devices with their start and end apart: 49, of which 25 were waited for; matrix products, arithmetic and copies ran while one was open for 2% of the time, Pallas kernels for 10%

profile of v1, /device:TPU:0, one launch (start us, length us, event | category | flops | bytes accessed | tf_op | source)
XLA Modules:
  0.0 191.1 jit_solution(4595854574795133191)
XLA Ops:
  2.6 3.1 %collective-permute-start.6 = (bf16[128,2048]{1,0:T(8,128)(2,1)S(1)}, bf16[128,2048]{1,0:T(8,128)(2,1)S(1)}, u32[]{:S(2)}, u32[]{:S(2)}) collective-permute-start(bf16[128,2048]{1,0:T(8,128)(2,1)S(1)} %get-tuple-element.56), channel_id=1, source_target_pairs={{0,1},{1,0},{2,3},{3,2},{4,5},{5,4},{6,7},{7,6},{8,9},{9,8},{10,11... | collective-permute-start | bytes 1572872 | tf_op jit(solution)/shard_map/ppermute | solution.py:261
  7.9 1.5 shard_map.93
  9.5 1.6 collective-permute-start.1
  11.7 1.5 collective-permute-start.18
  13.2 4.1 %collective-permute-done.1.refs_2_ = bf16[2,3,128,128]{3,2,1,0:T(8,128)(2,1)S(1)} collective-permute-done((bf16[2,3,128,128]{3,2,1,0:T(8,128)(2,1)S(1)}, bf16[2,3,128,128]{3,2,1,0:T(8,128)(2,1)S(1)}, u32[]{:S(2)}, u32[]{:S(2)}) %collective-permute-start.1) | collective-permute-done | bytes 196640 | tf_op jit(solution)/shard_map/ppermute | solution.py:261
  17.5 3.1 %collective-permute-done.2.refs_3_ = bf16[2,3,128,128]{3,2,1,0:T(8,128)(2,1)S(1)} collective-permute-done((bf16[2,3,128,128]{3,2,1,0:T(8,128)(2,1)S(1)}, bf16[2,3,128,128]{3,2,1,0:T(8,128)(2,1)S(1)}, u32[]{:S(2)}, u32[]{:S(2)}) %collective-permute-start.2) | collective-permute-done | bytes 196640 | tf_op jit(solution)/shard_map/ppermute | solution.py:261
  20.6 1.4 collective-permute-start.4
  22.6 3.2 %collective-permute-done.18.refs_2_ = bf16[2,3,128,128]{3,2,1,0:T(8,128)(2,1)S(1)} collective-permute-done((bf16[2,3,128,128]{3,2,1,0:T(8,128)(2,1)S(1)}, bf16[2,3,128,128]{3,2,1,0:T(8,128)(2,1)S(1)}, u32[]{:S(2)}, u32[]{:S(2)}) %collective-permute-start.18) | collective-permute-done | bytes 196640 | tf_op jit(solution)/shard_map/ppermute | solution.py:261
  25.8 1.5 collective-permute-start.28
  27.3 1.7 collective-permute-done.19.refs_3_
  29.0 1.9 collective-permute-start.29
  31.5 2.7 %collective-permute-start.30 = (bf16[256,512]{1,0:T(8,128)(2,1)S(1)}, bf16[256,512]{1,0:T(8,128)(2,1)S(1)}, u32[]{:S(2)}, u32[]{:S(2)}) collective-permute-start(bf16[256,512]{1,0:T(8,128)(2,1)S(1)} %get-tuple-element.98.refs_8_), channel_id=1, source_target_pairs={{0,4},{1,5},{2,6},{3,7},{4,0},{5,1},{6,2},{7,3},{8,12},{9,13},{10,... | collective-permute-start | bytes 786440 | tf_op jit(solution)/shard_map/ppermute | solution.py:261
  34.2 11.3 %collective-permute-done.28.refs_2_ = bf16[2,3,128,128]{3,2,1,0:T(8,128)(2,1)S(1)} collective-permute-done((bf16[2,3,128,128]{3,2,1,0:T(8,128)(2,1)S(1)}, bf16[2,3,128,128]{3,2,1,0:T(8,128)(2,1)S(1)}, u32[]{:S(2)}, u32[]{:S(2)}) %collective-permute-start.28) | collective-permute-done | bytes 196640 | tf_op jit(solution)/shard_map/ppermute | solution.py:261
  45.5 2.6 %collective-permute-start.10 = (bf16[256,512]{1,0:T(8,128)(2,1)S(1)}, bf16[256,512]{1,0:T(8,128)(2,1)S(1)}, u32[]{:S(2)}, u32[]{:S(2)}) collective-permute-start(bf16[256,512]{1,0:T(8,128)(2,1)S(1)} %get-tuple-element.99.refs_8_), channel_id=1, source_target_pairs={{0,4},{1,5},{2,6},{3,7},{4,0},{5,1},{6,2},{7,3},{8,12},{9,13},{10,... | collective-permute-start | bytes 786440 | tf_op jit(solution)/shard_map/ppermute | solution.py:261
  48.7 2.6 %collective-permute-start.20 = (bf16[256,512]{1,0:T(8,128)(2,1)S(1)}, bf16[256,512]{1,0:T(8,128)(2,1)S(1)}, u32[]{:S(2)}, u32[]{:S(2)}) collective-permute-start(bf16[256,512]{1,0:T(8,128)(2,1)S(1)} %get-tuple-element.100.refs_8_), channel_id=1, source_target_pairs={{0,4},{1,5},{2,6},{3,7},{4,0},{5,1},{6,2},{7,3},{8,12},{9,13},{10,... | collective-permute-start | bytes 786440 | tf_op jit(solution)/shard_map/ppermute | solution.py:261
  51.8 14.1 %collective-permute-done.10.refs_9_ = bf16[256,512]{1,0:T(8,128)(2,1)S(1)} collective-permute-done((bf16[256,512]{1,0:T(8,128)(2,1)S(1)}, bf16[256,512]{1,0:T(8,128)(2,1)S(1)}, u32[]{:S(2)}, u32[]{:S(2)}) %collective-permute-start.10) | collective-permute-done | bytes 262176 | tf_op jit(solution)/shard_map/ppermute | solution.py:261
  66.5 1.3 shard_map.102.refs_8_
  67.8 2.7 %collective-permute-done.20.refs_9_ = bf16[256,512]{1,0:T(8,128)(2,1)S(1)} collective-permute-done((bf16[256,512]{1,0:T(8,128)(2,1)S(1)}, bf16[256,512]{1,0:T(8,128)(2,1)S(1)}, u32[]{:S(2)}, u32[]{:S(2)}) %collective-permute-start.20) | collective-permute-done | bytes 262176 | tf_op jit(solution)/shard_map/ppermute | solution.py:261
  70.9 1.3 shard_map.104.refs_8_
  72.2 5.5 %collective-permute-done.37.refs_9_ = bf16[256,512]{1,0:T(8,128)(2,1)S(1)} collective-permute-done((bf16[256,512]{1,0:T(8,128)(2,1)S(1)}, bf16[256,512]{1,0:T(8,128)(2,1)S(1)}, u32[]{:S(2)}, u32[]{:S(2)}) %collective-permute-start.37) | collective-permute-done | bytes 262176 | tf_op jit(solution)/shard_map/ppermute | solution.py:261
  78.1 1.7 collective-permute-start.11
  80.2 1.3 shard_map.106.refs_8_
  81.4 1.8 collective-permute-start.21
  83.5 1.2 shard_map.103
  84.8 1.6 collective-permute-start.45
  86.4 1.2 shard_map.105
  87.7 1.7 collective-permute-start.31
  89.4 3.5 %collective-permute-done.12.refs_11_ = bf16[256,512]{1,0:T(8,128)(2,1)S(1)} collective-permute-done((bf16[256,512]{1,0:T(8,128)(2,1)S(1)}, bf16[256,512]{1,0:T(8,128)(2,1)S(1)}, u32[]{:S(2)}, u32[]{:S(2)}) %collective-permute-start.12) | collective-permute-done | bytes 262176 | tf_op jit(solution)/shard_map/ppermute | solution.py:261
  92.9 1.7 collective-permute-start.32
  94.7 1.3 shard_map.95
  95.9 2.6 %collective-permute-done.21.refs_10_ = bf16[256,512]{1,0:T(8,128)(2,1)S(1)} collective-permute-done((bf16[256,512]{1,0:T(8,128)(2,1)S(1)}, bf16[256,512]{1,0:T(8,128)(2,1)S(1)}, u32[]{:S(2)}, u32[]{:S(2)}) %collective-permute-start.21) | collective-permute-done | bytes 262176 | tf_op jit(solution)/shard_map/ppermute | solution.py:261
  98.6 1.6 collective-permute-start.13
  100.1 4.1 %collective-permute-done.22.refs_11_ = bf16[256,512]{1,0:T(8,128)(2,1)S(1)} collective-permute-done((bf16[256,512]{1,0:T(8,128)(2,1)S(1)}, bf16[256,512]{1,0:T(8,128)(2,1)S(1)}, u32[]{:S(2)}, u32[]{:S(2)}) %collective-permute-start.22) | collective-permute-done | bytes 262176 | tf_op jit(solution)/shard_map/ppermute | solution.py:261
  104.2 1.7 collective-permute-start.39
  105.9 1.3 shard_map.97
  107.2 1.6 collective-permute-start.23
  108.8 1.2 shard_map.107
  110.0 1.5 collective-permute-start.38
  111.5 3.9 %collective-permute-done.32.refs_11_ = bf16[256,512]{1,0:T(8,128)(2,1)S(1)} collective-permute-done((bf16[256,512]{1,0:T(8,128)(2,1)S(1)}, bf16[256,512]{1,0:T(8,128)(2,1)S(1)}, u32[]{:S(2)}, u32[]{:S(2)}) %collective-permute-start.32) | collective-permute-done | bytes 262176 | tf_op jit(solution)/shard_map/ppermute | solution.py:261
  115.4 1.7 collective-permute-start.43
  117.1 1.5 shard_map.99
  118.6 2.4 %collective-permute-done.39 = bf16[256,512]{1,0:T(8,128)(2,1)S(1)} collective-permute-done((bf16[256,512]{1,0:T(8,128)(2,1)S(1)}, bf16[256,512]{1,0:T(8,128)(2,1)S(1)}, u32[]{:S(2)}, u32[]{:S(2)}) %collective-permute-start.39) | collective-permute-done | bytes 262176 | tf_op jit(solution)/shard_map/ppermute | solution.py:261
  121.0 1.7 collective-permute-start.47
  122.8 9.4 %collective-permute-done.43 = bf16[256,512]{1,0:T(8,128)(2,1)S(1)} collective-permute-done((bf16[256,512]{1,0:T(8,128)(2,1)S(1)}, bf16[256,512]{1,0:T(8,128)(2,1)S(1)}, u32[]{:S(2)}, u32[]{:S(2)}) %collective-permute-start.43) | collective-permute-done | bytes 262176 | tf_op jit(solution)/shard_map/ppermute | solution.py:261
  132.3 3.6 %collective-permute-start.40 = (bf16[256,512]{1,0:T(8,128)(2,1)S(1)}, bf16[256,512]{1,0:T(8,128)(2,1)S(1)}, u32[]{:S(2)}, u32[]{:S(2)}) collective-permute-start(bf16[256,512]{1,0:T(8,128)(2,1)S(1)} %add_convert_fusion.2), channel_id=1, source_target_pairs={{0,4},{1,5},{2,6},{3,7},{4,0},{5,1},{6,2},{7,3},{8,12},{9,13},{10,... | collective-permute-start | bytes 786440 | tf_op jit(solution)/shard_map/ppermute | solution.py:261
  135.9 3.8 %collective-permute-done.47 = bf16[256,512]{1,0:T(8,128)(2,1)S(1)} collective-permute-done((bf16[256,512]{1,0:T(8,128)(2,1)S(1)}, bf16[256,512]{1,0:T(8,128)(2,1)S(1)}, u32[]{:S(2)}, u32[]{:S(2)}) %collective-permute-start.47) | collective-permute-done | bytes 262176 | tf_op jit(solution)/shard_map/ppermute | solution.py:261
  139.7 1.7 collective-permute-start.33
  141.6 4.0 %collective-permute-done.40 = bf16[256,512]{1,0:T(8,128)(2,1)S(1)} collective-permute-done((bf16[256,512]{1,0:T(8,128)(2,1)S(1)}, bf16[256,512]{1,0:T(8,128)(2,1)S(1)}, u32[]{:S(2)}, u32[]{:S(2)}) %collective-permute-start.40) | collective-permute-done | bytes 262176 | tf_op jit(solution)/shard_map/ppermute | solution.py:261
  145.6 3.0 %collective-permute-start.44 = (bf16[256,512]{1,0:T(8,128)(2,1)S(1)}, bf16[256,512]{1,0:T(8,128)(2,1)S(1)}, u32[]{:S(2)}, u32[]{:S(2)}) collective-permute-start(bf16[256,512]{1,0:T(8,128)(2,1)S(1)} %add_convert_fusion.1), channel_id=1, source_target_pairs={{0,4},{1,5},{2,6},{3,7},{4,0},{5,1},{6,2},{7,3},{8,12},{9,13},{10,... | collective-permute-start | bytes 786440 | tf_op jit(solution)/shard_map/ppermute | solution.py:261
  148.7 2.2 %shard_map.96 = (bf16[2,3,128,128]{3,2,1,0:T(8,128)(2,1)S(1)}, bf16[2,3,128,128]{3,2,1,0:T(8,128)(2,1)S(1)}, bf16[2,3,128,128]{3,2,1,0:T(8,128)(2,1)S(1)}, bf16[2,3,128,128]{3,2,1,0:T(8,128)(2,1)S(1)}) custom-call(bf16[2,3,128,128]{3,2,1,0:T(8,128)(2,1)S(1)} %get-tuple-element.51.refs_0_, bf16[2,3,128,128]{3,2,1,0:T(8,128)(2,1)S(1)} %collective-permute-done.refs_1_, ...), custom_call_target="tpu_custom_call" | custom-call | flops 805306368 | bytes 2621440 | tf_op jit(solution)/shard_map/pallas_call | solution.py:149
  150.9 2.1 %shard_map.98 = (bf16[2,3,128,128]{3,2,1,0:T(8,128)(2,1)S(1)}, bf16[2,3,128,128]{3,2,1,0:T(8,128)(2,1)S(1)}, bf16[2,3,128,128]{3,2,1,0:T(8,128)(2,1)S(1)}, bf16[2,3,128,128]{3,2,1,0:T(8,128)(2,1)S(1)}) custom-call(bf16[2,3,128,128]{3,2,1,0:T(8,128)(2,1)S(1)} %get-tuple-element.63.refs_0_, bf16[2,3,128,128]{3,2,1,0:T(8,128)(2,1)S(1)} %collective-permute-done.17.refs_1_, ...), custom_call_target="tpu_custom_call" | custom-call | flops 805306368 | bytes 2621440 | tf_op jit(solution)/shard_map/pallas_call | solution.py:149
  153.1 6.7 %collective-permute-done.42 = bf16[256,512]{1,0:T(8,128)(2,1)S(1)} collective-permute-done((bf16[256,512]{1,0:T(8,128)(2,1)S(1)}, bf16[256,512]{1,0:T(8,128)(2,1)S(1)}, u32[]{:S(2)}, u32[]{:S(2)}) %collective-permute-start.42) | collective-permute-done | bytes 262176 | tf_op jit(solution)/shard_map/ppermute | solution.py:261
  159.8 2.8 %collective-permute-done.46 = bf16[256,512]{1,0:T(8,128)(2,1)S(1)} collective-permute-done((bf16[256,512]{1,0:T(8,128)(2,1)S(1)}, bf16[256,512]{1,0:T(8,128)(2,1)S(1)}, u32[]{:S(2)}, u32[]{:S(2)}) %collective-permute-start.46) | collective-permute-done | bytes 262176 | tf_op jit(solution)/shard_map/ppermute | solution.py:261
  162.6 1.5 collective-permute-start.15
  164.8 2.1 %shard_map.100 = (bf16[2,3,128,128]{3,2,1,0:T(8,128)(2,1)S(1)}, bf16[2,3,128,128]{3,2,1,0:T(8,128)(2,1)S(1)}, bf16[2,3,128,128]{3,2,1,0:T(8,128)(2,1)S(1)}, bf16[2,3,128,128]{3,2,1,0:T(8,128)(2,1)S(1)}) custom-call(bf16[2,3,128,128]{3,2,1,0:T(8,128)(2,1)S(1)} %get-tuple-element.73.refs_0_, bf16[2,3,128,128]{3,2,1,0:T(8,128)(2,1)S(1)} %collective-permute-done.27.refs_1_, ...), custom_call_target="tpu_custom_call" | custom-call | flops 805306368 | bytes 2621440 | tf_op jit(solution)/shard_map/pallas_call | solution.py:149
  167.0 1.9 collective-permute-done.48
  168.9 1.5 collective-permute-start.25
  171.0 2.6 %collective-permute-done.16.refs_3_ = bf16[2,3,128,128]{3,2,1,0:T(8,128)(2,1)S(1)} collective-permute-done((bf16[2,3,128,128]{3,2,1,0:T(8,128)(2,1)S(1)}, bf16[2,3,128,128]{3,2,1,0:T(8,128)(2,1)S(1)}, u32[]{:S(2)}, u32[]{:S(2)}) %collective-permute-start.16) | collective-permute-done | bytes 196640 | tf_op jit(solution)/shard_map/ppermute | solution.py:261
  173.6 2.2 %collective-permute-start.36 = (bf16[2,3,128,128]{3,2,1,0:T(8,128)(2,1)S(1)}, bf16[2,3,128,128]{3,2,1,0:T(8,128)(2,1)S(1)}, u32[]{:S(2)}, u32[]{:S(2)}) collective-permute-start(bf16[2,3,128,128]{3,2,1,0:T(8,128)(2,1)S(1)} %get-tuple-element.82), channel_id=1, source_target_pairs={{0,24},{8,16},{16,8},{24,0},{1,25},{9,17},{17,9},{25,1},{2,26},{10... | collective-permute-start | bytes 589832 | tf_op jit(solution)/shard_map/ppermute | solution.py:261
  175.9 1.3 pad_maximum_fusion
  177.9 4.1 %collective-permute-done.26.refs_7_ = bf16[2,3,128,128]{3,2,1,0:T(8,128)(2,1)S(1)} collective-permute-done((bf16[2,3,128,128]{3,2,1,0:T(8,128)(2,1)S(1)}, bf16[2,3,128,128]{3,2,1,0:T(8,128)(2,1)S(1)}, u32[]{:S(2)}, u32[]{:S(2)}) %collective-permute-start.26) | collective-permute-done | bytes 196640 | tf_op jit(solution)/shard_map/ppermute | solution.py:261
  182.0 4.3 %collective-permute-done.35.refs_10_ = bf16[2,3,128,128]{3,2,1,0:T(8,128)(2,1)S(1)} collective-permute-done((bf16[2,3,128,128]{3,2,1,0:T(8,128)(2,1)S(1)}, bf16[2,3,128,128]{3,2,1,0:T(8,128)(2,1)S(1)}, u32[]{:S(2)}, u32[]{:S(2)}) %collective-permute-start.35) | collective-permute-done | bytes 196640 | tf_op jit(solution)/shard_map/ppermute | solution.py:261
  186.3 2.0 %collective-permute-done.36.refs_11_ = bf16[2,3,128,128]{3,2,1,0:T(8,128)(2,1)S(1)} collective-permute-done((bf16[2,3,128,128]{3,2,1,0:T(8,128)(2,1)S(1)}, bf16[2,3,128,128]{3,2,1,0:T(8,128)(2,1)S(1)}, u32[]{:S(2)}, u32[]{:S(2)}) %collective-permute-start.36) | collective-permute-done | bytes 196640 | tf_op jit(solution)/shard_map/ppermute | solution.py:261
  188.3 2.8 %shard_map.101 = (bf16[128,3072]{1,0:T(8,128)(2,1)}, bf16[128,3072]{1,0:T(8,128)(2,1)}, bf16[128,3072]{1,0:T(8,128)(2,1)}) custom-call(s32[2]{0:T(128)S(1)} %pad_add_fusion.at_ref.at, f32[128,128]{1,0:T(8,128)S(1)} %get-tuple-element.104.cos, f32[128,128]{1,0:T(8,128)S(1)} %get-tuple-element.105.sin, bf16[2,3,128,128]{3,2,1,0:T(8,128)(2,1)S(1)} %get-tuple-element.59.refs_0_, ...), custom_call_target="tpu_custom_call" | custom-call | bytes 4718592 | tf_op jit(solution)/shard_map/pallas_call | solution.py:230
  (72 shorter events, 12.3 us)
Async XLA Ops:
  0.7 1.2 copy-start
  1.9 4.8 %copy-start.1 = (bf16[1,128,3072]{2,1,0:T(8,128)(2,1)S(1)}, bf16[1,128,3072]{2,1,0:T(8,128)(2,1)}, u32[]{:S(2)}) copy-start(bf16[1,128,3072]{2,1,0:T(8,128)(2,1)} %param.6) | copy-start | bytes 2359300
  1.9 4.8 %copy-start.2 = (bf16[1,128,3072]{2,1,0:T(8,128)(2,1)S(1)}, bf16[1,128,3072]{2,1,0:T(8,128)(2,1)}, u32[]{:S(2)}) copy-start(bf16[1,128,3072]{2,1,0:T(8,128)(2,1)} %param.7) | copy-start | bytes 2359300
  2.6 28.3 %collective-permute-start.6 = (bf16[128,2048]{1,0:T(8,128)(2,1)S(1)}, bf16[128,2048]{1,0:T(8,128)(2,1)S(1)}, u32[]{:S(2)}, u32[]{:S(2)}) collective-permute-start(bf16[128,2048]{1,0:T(8,128)(2,1)S(1)} %get-tuple-element.56), channel_id=1, source_target_pairs={{0,1},{1,0},{2,3},{3,2},{4,5},{5,4},{6,7},{7,6},{8,9},{9,8},{10,11... | collective-permute-start | bytes 1572872 | tf_op jit(solution)/shard_map/ppermute | solution.py:261
  6.8 1.1 copy-start.3
  7.9 23.6 %copy-start.4 = (bf16[768,512]{1,0:T(8,128)(2,1)S(1)}, bf16[768,512]{1,0:T(8,128)(2,1)}, u32[]{:S(2)}) copy-start(bf16[768,512]{1,0:T(8,128)(2,1)} %param.11) | copy-start | bytes 2359300
  9.4 2.3 %collective-permute-start = (bf16[2,3,128,128]{3,2,1,0:T(8,128)(2,1)S(1)}, bf16[2,3,128,128]{3,2,1,0:T(8,128)(2,1)S(1)}, u32[]{:S(2)}, u32[]{:S(2)}) collective-permute-start(bf16[2,3,128,128]{3,2,1,0:T(8,128)(2,1)S(1)} %get-tuple-element.52), channel_id=1, source_target_pairs={{0,8},{8,0},{16,24},{24,16},{1,9},{9,1},{17,25},{25,17},{2,10},{10... | collective-permute-start | bytes 589832 | tf_op jit(solution)/shard_map/ppermute | solution.py:261
  9.5 7.8 %collective-permute-start.1 = (bf16[2,3,128,128]{3,2,1,0:T(8,128)(2,1)S(1)}, bf16[2,3,128,128]{3,2,1,0:T(8,128)(2,1)S(1)}, u32[]{:S(2)}, u32[]{:S(2)}) collective-permute-start(bf16[2,3,128,128]{3,2,1,0:T(8,128)(2,1)S(1)} %get-tuple-element.53), channel_id=1, source_target_pairs={{0,16},{8,24},{16,0},{24,8},{1,17},{9,25},{17,1},{25,9},{2,18},{10... | collective-permute-start | bytes 589832 | tf_op jit(solution)/shard_map/ppermute | solution.py:261
  11.1 9.5 %collective-permute-start.2 = (bf16[2,3,128,128]{3,2,1,0:T(8,128)(2,1)S(1)}, bf16[2,3,128,128]{3,2,1,0:T(8,128)(2,1)S(1)}, u32[]{:S(2)}, u32[]{:S(2)}) collective-permute-start(bf16[2,3,128,128]{3,2,1,0:T(8,128)(2,1)S(1)} %get-tuple-element.54), channel_id=1, source_target_pairs={{0,24},{8,16},{16,8},{24,0},{1,25},{9,17},{17,9},{25,1},{2,26},{10... | collective-permute-start | bytes 589832 | tf_op jit(solution)/shard_map/ppermute | solution.py:261
  11.4 10.6 %collective-permute-start.17 = (bf16[2,3,128,128]{3,2,1,0:T(8,128)(2,1)S(1)}, bf16[2,3,128,128]{3,2,1,0:T(8,128)(2,1)S(1)}, u32[]{:S(2)}, u32[]{:S(2)}) collective-permute-start(bf16[2,3,128,128]{3,2,1,0:T(8,128)(2,1)S(1)} %get-tuple-element.64), channel_id=1, source_target_pairs={{0,8},{8,0},{16,24},{24,16},{1,9},{9,1},{17,25},{25,17},{2,10},{10... | collective-permute-start | bytes 589832 | tf_op jit(solution)/shard_map/ppermute | solution.py:261
  11.7 14.1 %collective-permute-start.18 = (bf16[2,3,128,128]{3,2,1,0:T(8,128)(2,1)S(1)}, bf16[2,3,128,128]{3,2,1,0:T(8,128)(2,1)S(1)}, u32[]{:S(2)}, u32[]{:S(2)}) collective-permute-start(bf16[2,3,128,128]{3,2,1,0:T(8,128)(2,1)S(1)} %get-tuple-element.65), channel_id=1, source_target_pairs={{0,16},{8,24},{16,0},{24,8},{1,17},{9,25},{17,1},{25,9},{2,18},{10... | collective-permute-start | bytes 589832 | tf_op jit(solution)/shard_map/ppermute | solution.py:261
  17.4 11.6 %collective-permute-start.19 = (bf16[2,3,128,128]{3,2,1,0:T(8,128)(2,1)S(1)}, bf16[2,3,128,128]{3,2,1,0:T(8,128)(2,1)S(1)}, u32[]{:S(2)}, u32[]{:S(2)}) collective-permute-start(bf16[2,3,128,128]{3,2,1,0:T(8,128)(2,1)S(1)} %get-tuple-element.66), channel_id=1, source_target_pairs={{0,24},{8,16},{16,8},{24,0},{1,25},{9,17},{17,9},{25,1},{2,26},{10... | collective-permute-start | bytes 589832 | tf_op jit(solution)/shard_map/ppermute | solution.py:261
  20.6 45.4 %collective-permute-start.4 = (bf16[128,2048]{1,0:T(8,128)(2,1)S(1)}, bf16[128,2048]{1,0:T(8,128)(2,1)S(1)}, u32[]{:S(2)}, u32[]{:S(2)}) collective-permute-start(bf16[128,2048]{1,0:T(8,128)(2,1)S(1)} %get-tuple-element.55.refs_0_), channel_id=1, source_target_pairs={{0,16},{8,24},{16,0},{24,8},{1,17},{9,25},{17,1},{25,9},{2,18},{10... | collective-permute-start | bytes 1572872 | tf_op jit(solution)/shard_map/ppermute | solution.py:261
  22.0 9.5 %collective-permute-start.27 = (bf16[2,3,128,128]{3,2,1,0:T(8,128)(2,1)S(1)}, bf16[2,3,128,128]{3,2,1,0:T(8,128)(2,1)S(1)}, u32[]{:S(2)}, u32[]{:S(2)}) collective-permute-start(bf16[2,3,128,128]{3,2,1,0:T(8,128)(2,1)S(1)} %get-tuple-element.74), channel_id=1, source_target_pairs={{0,8},{8,0},{16,24},{24,16},{1,9},{9,1},{17,25},{25,17},{2,10},{10... | collective-permute-start | bytes 589832 | tf_op jit(solution)/shard_map/ppermute | solution.py:261
  25.8 19.7 %collective-permute-start.28 = (bf16[2,3,128,128]{3,2,1,0:T(8,128)(2,1)S(1)}, bf16[2,3,128,128]{3,2,1,0:T(8,128)(2,1)S(1)}, u32[]{:S(2)}, u32[]{:S(2)}) collective-permute-start(bf16[2,3,128,128]{3,2,1,0:T(8,128)(2,1)S(1)} %get-tuple-element.75), channel_id=1, source_target_pairs={{0,16},{8,24},{16,0},{24,8},{1,17},{9,25},{17,1},{25,9},{2,18},{10... | collective-permute-start | bytes 589832 | tf_op jit(solution)/shard_map/ppermute | solution.py:261
  29.0 19.7 %collective-permute-start.29 = (bf16[2,3,128,128]{3,2,1,0:T(8,128)(2,1)S(1)}, bf16[2,3,128,128]{3,2,1,0:T(8,128)(2,1)S(1)}, u32[]{:S(2)}, u32[]{:S(2)}) collective-permute-start(bf16[2,3,128,128]{3,2,1,0:T(8,128)(2,1)S(1)} %get-tuple-element.76), channel_id=1, source_target_pairs={{0,24},{8,16},{16,8},{24,0},{1,25},{9,17},{17,9},{25,1},{2,26},{10... | collective-permute-start | bytes 589832 | tf_op jit(solution)/shard_map/ppermute | solution.py:261
  30.9 35.5 %collective-permute-start.8 = (bf16[128,2048]{1,0:T(8,128)(2,1)S(1)}, bf16[128,2048]{1,0:T(8,128)(2,1)S(1)}, u32[]{:S(2)}, u32[]{:S(2)}) collective-permute-start(bf16[128,2048]{1,0:T(8,128)(2,1)S(1)} %collective-permute-done.6.refs_4_), channel_id=1, source_target_pairs={{0,16},{8,24},{16,0},{24,8},{1,17},{9,25},{17,1},{25,9},{2,18},{10... | collective-permute-start | bytes 1572872 | tf_op jit(solution)/shard_map/ppermute | solution.py:261
  31.5 19.7 %collective-permute-start.30 = (bf16[256,512]{1,0:T(8,128)(2,1)S(1)}, bf16[256,512]{1,0:T(8,128)(2,1)S(1)}, u32[]{:S(2)}, u32[]{:S(2)}) collective-permute-start(bf16[256,512]{1,0:T(8,128)(2,1)S(1)} %get-tuple-element.98.refs_8_), channel_id=1, source_target_pairs={{0,4},{1,5},{2,6},{3,7},{4,0},{5,1},{6,2},{7,3},{8,12},{9,13},{10,... | collective-permute-start | bytes 786440 | tf_op jit(solution)/shard_map/ppermute | solution.py:261
  45.5 20.5 %collective-permute-start.10 = (bf16[256,512]{1,0:T(8,128)(2,1)S(1)}, bf16[256,512]{1,0:T(8,128)(2,1)S(1)}, u32[]{:S(2)}, u32[]{:S(2)}) collective-permute-start(bf16[256,512]{1,0:T(8,128)(2,1)S(1)} %get-tuple-element.99.refs_8_), channel_id=1, source_target_pairs={{0,4},{1,5},{2,6},{3,7},{4,0},{5,1},{6,2},{7,3},{8,12},{9,13},{10,... | collective-permute-start | bytes 786440 | tf_op jit(solution)/shard_map/ppermute | solution.py:261
  48.7 21.8 %collective-permute-start.20 = (bf16[256,512]{1,0:T(8,128)(2,1)S(1)}, bf16[256,512]{1,0:T(8,128)(2,1)S(1)}, u32[]{:S(2)}, u32[]{:S(2)}) collective-permute-start(bf16[256,512]{1,0:T(8,128)(2,1)S(1)} %get-tuple-element.100.refs_8_), channel_id=1, source_target_pairs={{0,4},{1,5},{2,6},{3,7},{4,0},{5,1},{6,2},{7,3},{8,12},{9,13},{10,... | collective-permute-start | bytes 786440 | tf_op jit(solution)/shard_map/ppermute | solution.py:261
  51.3 26.9 %collective-permute-start.3 = (bf16[128,2048]{1,0:T(8,128)(2,1)S(1)}, bf16[128,2048]{1,0:T(8,128)(2,1)S(1)}, u32[]{:S(2)}, u32[]{:S(2)}) collective-permute-start(bf16[128,2048]{1,0:T(8,128)(2,1)S(1)} %get-tuple-element.55.refs_0_), channel_id=1, source_target_pairs={{0,8},{8,0},{16,24},{24,16},{1,9},{9,1},{17,25},{25,17},{2,10},{10... | collective-permute-start | bytes 1572872 | tf_op jit(solution)/shard_map/ppermute | solution.py:261
  65.9 13.9 %collective-permute-start.7 = (bf16[128,2048]{1,0:T(8,128)(2,1)S(1)}, bf16[128,2048]{1,0:T(8,128)(2,1)S(1)}, u32[]{:S(2)}, u32[]{:S(2)}) collective-permute-start(bf16[128,2048]{1,0:T(8,128)(2,1)S(1)} %collective-permute-done.6.refs_4_), channel_id=1, source_target_pairs={{0,8},{8,0},{16,24},{24,16},{1,9},{9,1},{17,25},{25,17},{2,10},{10... | collective-permute-start | bytes 1572872 | tf_op jit(solution)/shard_map/ppermute | solution.py:261
  65.9 15.5 %collective-permute-start.5 = (bf16[128,2048]{1,0:T(8,128)(2,1)S(1)}, bf16[128,2048]{1,0:T(8,128)(2,1)S(1)}, u32[]{:S(2)}, u32[]{:S(2)}) collective-permute-start(bf16[128,2048]{1,0:T(8,128)(2,1)S(1)} %collective-permute-done.4.refs_2_), channel_id=1, source_target_pairs={{0,8},{8,0},{16,24},{24,16},{1,9},{9,1},{17,25},{25,17},{2,10},{10... | collective-permute-start | bytes 1572872 | tf_op jit(solution)/shard_map/ppermute | solution.py:261
  66.4 16.8 %collective-permute-start.9 = (bf16[128,2048]{1,0:T(8,128)(2,1)S(1)}, bf16[128,2048]{1,0:T(8,128)(2,1)S(1)}, u32[]{:S(2)}, u32[]{:S(2)}) collective-permute-start(bf16[128,2048]{1,0:T(8,128)(2,1)S(1)} %collective-permute-done.8.refs_6_), channel_id=1, source_target_pairs={{0,8},{8,0},{16,24},{24,16},{1,9},{9,1},{17,25},{25,17},{2,10},{10... | collective-permute-start | bytes 1572872 | tf_op jit(solution)/shard_map/ppermute | solution.py:261
  70.4 7.2 %collective-permute-start.37 = (bf16[256,512]{1,0:T(8,128)(2,1)S(1)}, bf16[256,512]{1,0:T(8,128)(2,1)S(1)}, u32[]{:S(2)}, u32[]{:S(2)}) collective-permute-start(bf16[256,512]{1,0:T(8,128)(2,1)S(1)} %shard_map.102.refs_8_), channel_id=1, source_target_pairs={{0,1},{1,0},{2,3},{3,2},{4,5},{5,4},{6,7},{7,6},{8,9},{9,8},{10,11... | collective-permute-start | bytes 786440 | tf_op jit(solution)/shard_map/ppermute | solution.py:261
  77.7 7.1 %collective-permute-start.41 = (bf16[256,512]{1,0:T(8,128)(2,1)S(1)}, bf16[256,512]{1,0:T(8,128)(2,1)S(1)}, u32[]{:S(2)}, u32[]{:S(2)}) collective-permute-start(bf16[256,512]{1,0:T(8,128)(2,1)S(1)} %shard_map.104.refs_8_), channel_id=1, source_target_pairs={{0,1},{1,0},{2,3},{3,2},{4,5},{5,4},{6,7},{7,6},{8,9},{9,8},{10,11... | collective-permute-start | bytes 786440 | tf_op jit(solution)/shard_map/ppermute | solution.py:261
  78.1 9.5 %collective-permute-start.11 = (bf16[256,512]{1,0:T(8,128)(2,1)S(1)}, bf16[256,512]{1,0:T(8,128)(2,1)S(1)}, u32[]{:S(2)}, u32[]{:S(2)}) collective-permute-start(bf16[256,512]{1,0:T(8,128)(2,1)S(1)} %get-tuple-element.99.refs_8_), channel_id=1, source_target_pairs={{0,2},{1,3},{2,0},{3,1},{4,6},{5,7},{6,4},{7,5},{8,10},{9,11},{10,... | collective-permute-start | bytes 786440 | tf_op jit(solution)/shard_map/ppermute | solution.py:261
  79.9 13.1 %collective-permute-start.12 = (bf16[256,512]{1,0:T(8,128)(2,1)S(1)}, bf16[256,512]{1,0:T(8,128)(2,1)S(1)}, u32[]{:S(2)}, u32[]{:S(2)}) collective-permute-start(bf16[256,512]{1,0:T(8,128)(2,1)S(1)} %collective-permute-done.10.refs_9_), channel_id=1, source_target_pairs={{0,2},{1,3},{2,0},{3,1},{4,6},{5,7},{6,4},{7,5},{8,10},{9,11},{10,... | collective-permute-start | bytes 786440 | tf_op jit(solution)/shard_map/ppermute | solution.py:261
  81.4 17.1 %collective-permute-start.21 = (bf16[256,512]{1,0:T(8,128)(2,1)S(1)}, bf16[256,512]{1,0:T(8,128)(2,1)S(1)}, u32[]{:S(2)}, u32[]{:S(2)}) collective-permute-start(bf16[256,512]{1,0:T(8,128)(2,1)S(1)} %get-tuple-element.100.refs_8_), channel_id=1, source_target_pairs={{0,2},{1,3},{2,0},{3,1},{4,6},{5,7},{6,4},{7,5},{8,10},{9,11},{10,... | collective-permute-start | bytes 786440 | tf_op jit(solution)/shard_map/ppermute | solution.py:261
  83.2 20.9 %collective-permute-start.22 = (bf16[256,512]{1,0:T(8,128)(2,1)S(1)}, bf16[256,512]{1,0:T(8,128)(2,1)S(1)}, u32[]{:S(2)}, u32[]{:S(2)}) collective-permute-start(bf16[256,512]{1,0:T(8,128)(2,1)S(1)} %collective-permute-done.20.refs_9_), channel_id=1, source_target_pairs={{0,2},{1,3},{2,0},{3,1},{4,6},{5,7},{6,4},{7,5},{8,10},{9,11},{10,... | collective-permute-start | bytes 786440 | tf_op jit(solution)/shard_map/ppermute | solution.py:261
  84.8 22.4 %collective-permute-start.45 = (bf16[256,512]{1,0:T(8,128)(2,1)S(1)}, bf16[256,512]{1,0:T(8,128)(2,1)S(1)}, u32[]{:S(2)}, u32[]{:S(2)}) collective-permute-start(bf16[256,512]{1,0:T(8,128)(2,1)S(1)} %shard_map.106.refs_8_), channel_id=1, source_target_pairs={{0,1},{1,0},{2,3},{3,2},{4,5},{5,4},{6,7},{7,6},{8,9},{9,8},{10,11... | collective-permute-start | bytes 786440 | tf_op jit(solution)/shard_map/ppermute | solution.py:261
  87.7 22.3 %collective-permute-start.31 = (bf16[256,512]{1,0:T(8,128)(2,1)S(1)}, bf16[256,512]{1,0:T(8,128)(2,1)S(1)}, u32[]{:S(2)}, u32[]{:S(2)}) collective-permute-start(bf16[256,512]{1,0:T(8,128)(2,1)S(1)} %get-tuple-element.98.refs_8_), channel_id=1, source_target_pairs={{0,2},{1,3},{2,0},{3,1},{4,6},{5,7},{6,4},{7,5},{8,10},{9,11},{10,... | collective-permute-start | bytes 786440 | tf_op jit(solution)/shard_map/ppermute | solution.py:261
  92.9 22.5 %collective-permute-start.32 = (bf16[256,512]{1,0:T(8,128)(2,1)S(1)}, bf16[256,512]{1,0:T(8,128)(2,1)S(1)}, u32[]{:S(2)}, u32[]{:S(2)}) collective-permute-start(bf16[256,512]{1,0:T(8,128)(2,1)S(1)} %collective-permute-done.30.refs_9_), channel_id=1, source_target_pairs={{0,2},{1,3},{2,0},{3,1},{4,6},{5,7},{6,4},{7,5},{8,10},{9,11},{10,... | collective-permute-start | bytes 786440 | tf_op jit(solution)/shard_map/ppermute | solution.py:261
  98.6 47.1 %collective-permute-start.13 = (f32[512,256]{1,0:T(8,128)S(1)}, f32[512,256]{1,0:T(8,128)S(1)}, u32[]{:S(2)}, u32[]{:S(2)}) collective-permute-start(f32[512,256]{1,0:T(8,128)S(1)} %get-tuple-element.58), channel_id=1, source_target_pairs={{0,1},{1,0},{2,3},{3,2},{4,5},{5,4},{6,7},{7,6},{8,9},{9,8},{10,11... | collective-permute-start | bytes 1572872 | tf_op jit(solution)/shard_map/ppermute | solution.py:261
  104.2 16.9 %collective-permute-start.39 = (bf16[256,512]{1,0:T(8,128)(2,1)S(1)}, bf16[256,512]{1,0:T(8,128)(2,1)S(1)}, u32[]{:S(2)}, u32[]{:S(2)}) collective-permute-start(bf16[256,512]{1,0:T(8,128)(2,1)S(1)} %get-tuple-element.89), channel_id=1, source_target_pairs={{0,2},{1,3},{2,0},{3,1},{4,6},{5,7},{6,4},{7,5},{8,10},{9,11},{10,... | collective-permute-start | bytes 786440 | tf_op jit(solution)/shard_map/ppermute | solution.py:261
  107.2 43.7 %collective-permute-start.23 = (f32[512,256]{1,0:T(8,128)S(1)}, f32[512,256]{1,0:T(8,128)S(1)}, u32[]{:S(2)}, u32[]{:S(2)}) collective-permute-start(f32[512,256]{1,0:T(8,128)S(1)} %get-tuple-element.68), channel_id=1, source_target_pairs={{0,1},{1,0},{2,3},{3,2},{4,5},{5,4},{6,7},{7,6},{8,9},{9,8},{10,11... | collective-permute-start | bytes 1572872 | tf_op jit(solution)/shard_map/ppermute | solution.py:261
  110.0 31.5 %collective-permute-start.38 = (bf16[256,512]{1,0:T(8,128)(2,1)S(1)}, bf16[256,512]{1,0:T(8,128)(2,1)S(1)}, u32[]{:S(2)}, u32[]{:S(2)}) collective-permute-start(bf16[256,512]{1,0:T(8,128)(2,1)S(1)} %get-tuple-element.87), channel_id=1, source_target_pairs={{0,2},{1,3},{2,0},{3,1},{4,6},{5,7},{6,4},{7,5},{8,10},{9,11},{10,... | collective-permute-start | bytes 786440 | tf_op jit(solution)/shard_map/ppermute | solution.py:261
  115.4 16.9 %collective-permute-start.43 = (bf16[256,512]{1,0:T(8,128)(2,1)S(1)}, bf16[256,512]{1,0:T(8,128)(2,1)S(1)}, u32[]{:S(2)}, u32[]{:S(2)}) collective-permute-start(bf16[256,512]{1,0:T(8,128)(2,1)S(1)} %get-tuple-element.93), channel_id=1, source_target_pairs={{0,2},{1,3},{2,0},{3,1},{4,6},{5,7},{6,4},{7,5},{8,10},{9,11},{10,... | collective-permute-start | bytes 786440 | tf_op jit(solution)/shard_map/ppermute | solution.py:261
  121.0 18.7 %collective-permute-start.47 = (bf16[256,512]{1,0:T(8,128)(2,1)S(1)}, bf16[256,512]{1,0:T(8,128)(2,1)S(1)}, u32[]{:S(2)}, u32[]{:S(2)}) collective-permute-start(bf16[256,512]{1,0:T(8,128)(2,1)S(1)} %get-tuple-element.97), channel_id=1, source_target_pairs={{0,2},{1,3},{2,0},{3,1},{4,6},{5,7},{6,4},{7,5},{8,10},{9,11},{10,... | collective-permute-start | bytes 786440 | tf_op jit(solution)/shard_map/ppermute | solution.py:261
  132.3 13.4 %collective-permute-start.40 = (bf16[256,512]{1,0:T(8,128)(2,1)S(1)}, bf16[256,512]{1,0:T(8,128)(2,1)S(1)}, u32[]{:S(2)}, u32[]{:S(2)}) collective-permute-start(bf16[256,512]{1,0:T(8,128)(2,1)S(1)} %add_convert_fusion.2), channel_id=1, source_target_pairs={{0,4},{1,5},{2,6},{3,7},{4,0},{5,1},{6,2},{7,3},{8,12},{9,13},{10,... | collective-permute-start | bytes 786440 | tf_op jit(solution)/shard_map/ppermute | solution.py:261
  139.7 24.3 %collective-permute-start.33 = (f32[512,256]{1,0:T(8,128)S(1)}, f32[512,256]{1,0:T(8,128)S(1)}, u32[]{:S(2)}, u32[]{:S(2)}) collective-permute-start(f32[512,256]{1,0:T(8,128)S(1)} %get-tuple-element.78), channel_id=1, source_target_pairs={{0,1},{1,0},{2,3},{3,2},{4,5},{5,4},{6,7},{7,6},{8,9},{9,8},{10,11... | collective-permute-start | bytes 1572872 | tf_op jit(solution)/shard_map/ppermute | solution.py:261
  141.6 18.2 %collective-permute-start.42 = (bf16[256,512]{1,0:T(8,128)(2,1)S(1)}, bf16[256,512]{1,0:T(8,128)(2,1)S(1)}, u32[]{:S(2)}, u32[]{:S(2)}) collective-permute-start(bf16[256,512]{1,0:T(8,128)(2,1)S(1)} %get-tuple-element.91), channel_id=1, source_target_pairs={{0,2},{1,3},{2,0},{3,1},{4,6},{5,7},{6,4},{7,5},{8,10},{9,11},{10,... | collective-permute-start | bytes 786440 | tf_op jit(solution)/shard_map/ppermute | solution.py:261
  145.6 17.0 %collective-permute-start.46 = (bf16[256,512]{1,0:T(8,128)(2,1)S(1)}, bf16[256,512]{1,0:T(8,128)(2,1)S(1)}, u32[]{:S(2)}, u32[]{:S(2)}) collective-permute-start(bf16[256,512]{1,0:T(8,128)(2,1)S(1)} %get-tuple-element.95), channel_id=1, source_target_pairs={{0,2},{1,3},{2,0},{3,1},{4,6},{5,7},{6,4},{7,5},{8,10},{9,11},{10,... | collective-permute-start | bytes 786440 | tf_op jit(solution)/shard_map/ppermute | solution.py:261
  145.6 18.4 %collective-permute-start.44 = (bf16[256,512]{1,0:T(8,128)(2,1)S(1)}, bf16[256,512]{1,0:T(8,128)(2,1)S(1)}, u32[]{:S(2)}, u32[]{:S(2)}) collective-permute-start(bf16[256,512]{1,0:T(8,128)(2,1)S(1)} %add_convert_fusion.1), channel_id=1, source_target_pairs={{0,4},{1,5},{2,6},{3,7},{4,0},{5,1},{6,2},{7,3},{8,12},{9,13},{10,... | collective-permute-start | bytes 786440 | tf_op jit(solution)/shard_map/ppermute | solution.py:261
  150.9 18.0 %collective-permute-start.48 = (bf16[256,512]{1,0:T(8,128)(2,1)S(1)}, bf16[256,512]{1,0:T(8,128)(2,1)S(1)}, u32[]{:S(2)}, u32[]{:S(2)}) collective-permute-start(bf16[256,512]{1,0:T(8,128)(2,1)S(1)} %add_convert_fusion), channel_id=1, source_target_pairs={{0,4},{1,5},{2,6},{3,7},{4,0},{5,1},{6,2},{7,3},{8,12},{9,13},{10,... | collective-permute-start | bytes 786440 | tf_op jit(solution)/shard_map/ppermute | solution.py:261
  159.8 10.6 %collective-permute-start.14 = (bf16[2,3,128,128]{3,2,1,0:T(8,128)(2,1)S(1)}, bf16[2,3,128,128]{3,2,1,0:T(8,128)(2,1)S(1)}, u32[]{:S(2)}, u32[]{:S(2)}) collective-permute-start(bf16[2,3,128,128]{3,2,1,0:T(8,128)(2,1)S(1)} %get-tuple-element.60), channel_id=1, source_target_pairs={{0,8},{8,0},{16,24},{24,16},{1,9},{9,1},{17,25},{25,17},{2,10},{10... | collective-permute-start | bytes 589832 | tf_op jit(solution)/shard_map/ppermute | solution.py:261
  162.6 7.8 %collective-permute-start.15 = (bf16[2,3,128,128]{3,2,1,0:T(8,128)(2,1)S(1)}, bf16[2,3,128,128]{3,2,1,0:T(8,128)(2,1)S(1)}, u32[]{:S(2)}, u32[]{:S(2)}) collective-permute-start(bf16[2,3,128,128]{3,2,1,0:T(8,128)(2,1)S(1)} %get-tuple-element.61), channel_id=1, source_target_pairs={{0,16},{8,24},{16,0},{24,8},{1,17},{9,25},{17,1},{25,9},{2,18},{10... | collective-permute-start | bytes 589832 | tf_op jit(solution)/shard_map/ppermute | solution.py:261
  164.1 9.5 %collective-permute-start.16 = (bf16[2,3,128,128]{3,2,1,0:T(8,128)(2,1)S(1)}, bf16[2,3,128,128]{3,2,1,0:T(8,128)(2,1)S(1)}, u32[]{:S(2)}, u32[]{:S(2)}) collective-permute-start(bf16[2,3,128,128]{3,2,1,0:T(8,128)(2,1)S(1)} %get-tuple-element.62), channel_id=1, source_target_pairs={{0,24},{8,16},{16,8},{24,0},{1,25},{9,17},{17,9},{25,1},{2,26},{10... | collective-permute-start | bytes 589832 | tf_op jit(solution)/shard_map/ppermute | solution.py:261
  164.1 9.5 %collective-permute-start.24 = (bf16[2,3,128,128]{3,2,1,0:T(8,128)(2,1)S(1)}, bf16[2,3,128,128]{3,2,1,0:T(8,128)(2,1)S(1)}, u32[]{:S(2)}, u32[]{:S(2)}) collective-permute-start(bf16[2,3,128,128]{3,2,1,0:T(8,128)(2,1)S(1)} %get-tuple-element.70), channel_id=1, source_target_pairs={{0,8},{8,0},{16,24},{24,16},{1,9},{9,1},{17,25},{25,17},{2,10},{10... | collective-permute-start | bytes 589832 | tf_op jit(solution)/shard_map/ppermute | solution.py:261
  168.9 9.0 %collective-permute-start.25 = (bf16[2,3,128,128]{3,2,1,0:T(8,128)(2,1)S(1)}, bf16[2,3,128,128]{3,2,1,0:T(8,128)(2,1)S(1)}, u32[]{:S(2)}, u32[]{:S(2)}) collective-permute-start(bf16[2,3,128,128]{3,2,1,0:T(8,128)(2,1)S(1)} %get-tuple-element.71), channel_id=1, source_target_pairs={{0,16},{8,24},{16,0},{24,8},{1,17},{9,25},{17,1},{25,9},{2,18},{10... | collective-permute-start | bytes 589832 | tf_op jit(solution)/shard_map/ppermute | solution.py:261
  170.3 11.7 %collective-permute-start.26 = (bf16[2,3,128,128]{3,2,1,0:T(8,128)(2,1)S(1)}, bf16[2,3,128,128]{3,2,1,0:T(8,128)(2,1)S(1)}, u32[]{:S(2)}, u32[]{:S(2)}) collective-permute-start(bf16[2,3,128,128]{3,2,1,0:T(8,128)(2,1)S(1)} %get-tuple-element.72), channel_id=1, source_target_pairs={{0,24},{8,16},{16,8},{24,0},{1,25},{9,17},{17,9},{25,1},{2,26},{10... | collective-permute-start | bytes 589832 | tf_op jit(solution)/shard_map/ppermute | solution.py:261
  170.4 11.7 %collective-permute-start.34 = (bf16[2,3,128,128]{3,2,1,0:T(8,128)(2,1)S(1)}, bf16[2,3,128,128]{3,2,1,0:T(8,128)(2,1)S(1)}, u32[]{:S(2)}, u32[]{:S(2)}) collective-permute-start(bf16[2,3,128,128]{3,2,1,0:T(8,128)(2,1)S(1)} %get-tuple-element.80), channel_id=1, source_target_pairs={{0,8},{8,0},{16,24},{24,16},{1,9},{9,1},{17,25},{25,17},{2,10},{10... | collective-permute-start | bytes 589832 | tf_op jit(solution)/shard_map/ppermute | solution.py:261
  173.6 12.7 %collective-permute-start.35 = (bf16[2,3,128,128]{3,2,1,0:T(8,128)(2,1)S(1)}, bf16[2,3,128,128]{3,2,1,0:T(8,128)(2,1)S(1)}, u32[]{:S(2)}, u32[]{:S(2)}) collective-permute-start(bf16[2,3,128,128]{3,2,1,0:T(8,128)(2,1)S(1)} %get-tuple-element.81), channel_id=1, source_target_pairs={{0,16},{8,24},{16,0},{24,8},{1,17},{9,25},{17,1},{25,9},{2,18},{10... | collective-permute-start | bytes 589832 | tf_op jit(solution)/shard_map/ppermute | solution.py:261
  173.6 14.7 %collective-permute-start.36 = (bf16[2,3,128,128]{3,2,1,0:T(8,128)(2,1)S(1)}, bf16[2,3,128,128]{3,2,1,0:T(8,128)(2,1)S(1)}, u32[]{:S(2)}, u32[]{:S(2)}) collective-permute-start(bf16[2,3,128,128]{3,2,1,0:T(8,128)(2,1)S(1)} %get-tuple-element.82), channel_id=1, source_target_pairs={{0,24},{8,16},{16,8},{24,0},{1,25},{9,17},{17,9},{25,1},{2,26},{10... | collective-permute-start | bytes 589832 | tf_op jit(solution)/shard_map/ppermute | solution.py:261
